TPU v7x, 32 devices: a whole 2x2x4 slice. The times are simulated.
32 devices in a mesh: dp: 8 (over z, x), seq: 4 (over y, core).
Axes of the slice: x: 2, y: 2, z: 4, core: 2. Of those that a mesh axis runs over, the one named last changes fastest.
Arguments:
- captions: bfloat16 [96, 128, 768], P(('dp', 'seq')), may hold values from -6 to 6
- images: bfloat16 [96, 196, 768], P('dp'), may hold values from -6 to 6
- tissue_mask: int32 [96, 196], P('dp'), may hold values from 0 to 1, as said below
- gain_self: bfloat16 [768], P(('dp', 'seq')), may hold values from 0.5 to 1.5
- gain_cross: bfloat16 [768], P(('dp', 'seq')), may hold values from 0.5 to 1.5
- gain_mlp: bfloat16 [768], P(('dp', 'seq')), may hold values from 0.5 to 1.5
- w_qkv: bfloat16 [768, 2304], P(('dp', 'seq')), may hold values from -0.21875 to 0.21875
- w_self_out: bfloat16 [768, 768], P(('dp', 'seq')), may hold values from -0.625 to 0.625
- w_cross_q: bfloat16 [768, 768], P(('dp', 'seq')), may hold values from -0.21875 to 0.21875
- w_cross_kv: bfloat16 [768, 1536], P(('dp', 'seq')), may hold values from -0.21875 to 0.21875
- w_cross_out: bfloat16 [768, 768], P(('dp', 'seq')), may hold values from -0.625 to 0.625
- w_up: bfloat16 [768, 3072], P(('dp', 'seq')), may hold values from -0.21875 to 0.21875
- w_down: bfloat16 [3072, 768], P(('dp', 'seq')), may hold values from -0.109375 to 0.109375
- cotangent: bfloat16 [96, 128, 768], P(('dp', 'seq')), may hold values from -6 to 6
Outputs:
- block_out: bfloat16 [96, 128, 768], P(('dp', 'seq'))
- grad_captions: float32 [96, 128, 768], P(('dp', 'seq'))
- grad_images: float32 [96, 196, 768], P('dp', None, 'seq')
- grad_gain_self: float32 [768], P(('dp', 'seq'))
- grad_gain_cross: float32 [768], P(('dp', 'seq'))
- grad_gain_mlp: float32 [768], P(('dp', 'seq'))
- grad_w_qkv: float32 [768, 2304], P(('dp', 'seq'))
- grad_w_self_out: float32 [768, 768], P(('dp', 'seq'))
- grad_w_cross_q: float32 [768, 768], P(('dp', 'seq'))
- grad_w_cross_kv: float32 [768, 1536], P(('dp', 'seq'))
- grad_w_cross_out: float32 [768, 768], P(('dp', 'seq'))
- grad_w_up: float32 [768, 3072], P(('dp', 'seq'))
- grad_w_down: float32 [3072, 768], P(('dp', 'seq'))
Inputs may be any that keep to these rules, and one draw needn't show every extreme that they name: `tissue_mask`: at least 65 of every image's patches are valid; the valid ones lie anywhere among its 196 slots and their number differs from image to image.
All inputs are finite; a program needn't handle non-finite values.
Results may differ from a plain program's by a relative error of at most 0.019.
Values may be sent and summed in bfloat16 or wider, within the bound.
A program may use at most 192 MiB of HBM per device.

v0:
```python
import functools

import jax
import jax.numpy as jnp
from jax import lax
from jax.experimental import pallas as pl
from jax.experimental.pallas import tpu as pltpu
from jax.sharding import PartitionSpec as P

HEADS = 12
HEAD = 64
EPS = 1e-05
BOTH = ("dp", "seq")
f32 = jnp.float32
bf16 = jnp.bfloat16
MESH = pl.DeviceIdType.MESH
HBM = pltpu.MemorySpace.HBM
VMEM = pltpu.MemorySpace.VMEM
LANES = 128


class Place:
    def __init__(self, nz, wide=False):
        dp, seq = lax.axis_index("dp"), lax.axis_index("seq")
        self.nz = nz
        self.z, self.x = dp // 2, lax.rem(dp, 2)
        self.y, self.c = seq // 2, lax.rem(seq, 2)
        x, y = self.x, self.y
        self.role = role = 1 if wide else self.c
        self.p = x + role * (y - x)
        self.s = y + role * (x - y)
        self.sib = (dp, 2 * y + (1 - self.c))
        self.p_xy = (x + (1 - role) * (1 - 2 * x), y + role * (1 - 2 * y))
        self.s_xy = (x + role * (1 - 2 * x), y + (1 - role) * (1 - 2 * y))
        self.ps_xy = (1 - x, 1 - y)
        self.p_dev = self.dev(self.z, self.p_xy)
        self.s_dev = self.dev(self.z, self.s_xy)
        self.z_of = [lax.rem(self.z + k, nz) for k in range(nz)]
        self.z_devs = [self.dev(self.z_of[k], (x, y)) for k in range(nz)]

    def dev(self, z, xy):
        return (2 * z + xy[0], 2 * xy[1] + self.c)

    def column(self, p, s):
        return p + self.role * (s - p), s + self.role * (p - s)

    def partners(self):
        return [*self.z_devs[1:], self.p_dev, self.s_dev, self.sib]


def enter(partners):
    barrier = pltpu.get_barrier_semaphore()
    for d in partners:
        pl.semaphore_signal(barrier, inc=1, device_id=d, device_id_type=MESH)
    pl.semaphore_wait(barrier, len(partners))


def remote(src, dst, sems, i, dev):
    return pltpu.make_async_remote_copy(
        src_ref=src, dst_ref=dst, send_sem=sems[0].at[i], recv_sem=sems[1].at[i],
        device_id=dev, device_id_type=MESH,
    )


class Gather:
    LOADS = (("z", 8), ("xy", 8), ("xy", 4), ("core", 8), None)
    WORK = (0.3, 0.3, 0.2, 0.2, 0.1)

    def __init__(self, here, shard, full, sems, local):
        h = here
        x, y, c = h.x, h.y, h.c
        mine = full.at[h.z, x, y, c]

        def col(xy):
            return full.at[:, xy[0], xy[1], c]

        self.own = pltpu.make_async_copy(shard, mine, local)
        nz = h.nz
        self.zs = [remote(shard, mine, sems, k - 1, h.z_devs[k]) for k in range(1, nz)]
        own, px, sx, psx = (x, y), h.p_xy, h.s_xy, h.ps_xy
        n = nz - 1
        self.p_own = remote(col(own), col(own), sems, n, h.p_dev)
        self.s_own = remote(col(own), col(own), sems, n + 1, h.s_dev)
        self.s_p = remote(col(px), col(px), sems, n + 2, h.s_dev)
        self.sibs = [
            remote(col(xy), col(xy), sems, n + 3 + i, h.sib)
            for i, xy in enumerate((own, px, sx, psx))
        ]

    @staticmethod
    def count(nz):
        return nz + 6

    def step(self, i):
        if i == 0:
            self.own.start()
            for t in self.zs:
                t.start()
        elif i == 1:
            self.own.wait()
            for t in self.zs:
                t.wait_recv()
            self.p_own.start()
            self.s_own.start()
            self.sibs[0].start()
        elif i == 2:
            self.p_own.wait_recv()
            self.s_p.start()
            self.sibs[1].start()
        elif i == 3:
            self.s_own.wait_recv()
            self.sibs[2].start()
            self.s_p.wait_recv()
            self.sibs[3].start()
        elif i == 4:
            for t in self.sibs:
                t.wait_recv()
        elif i == 5:
            for t in (*self.zs, self.p_own, self.s_own, self.s_p, *self.sibs):
                t.wait_send()


class GatherPlane(Gather):
    LOADS = (("xy", 2), ("xy", 1), ("z", 32), ("core", 12), None)

    def __init__(self, here, shard, full, sems, local):
        h = here
        x, y, c, z = h.x, h.y, h.c, h.z
        mine = full.at[z, x, y, c]
        pb = full.at[z, h.p_xy[0], h.p_xy[1], c]

        def plane(i):
            return full.at[i, :, :, c]

        self.own = pltpu.make_async_copy(shard, mine, local)
        nz = h.nz
        self.p_own = remote(shard, mine, sems, 0, h.p_dev)
        self.s_own = remote(shard, mine, sems, 1, h.s_dev)
        self.s_p = remote(pb, pb, sems, 2, h.s_dev)
        self.zs = [remote(plane(z), plane(z), sems, 2 + k, h.z_devs[k]) for k in range(1, nz)]
        self.sibs = [
            remote(plane(h.z_of[-k]), plane(h.z_of[-k]), sems, 2 + nz + k, h.sib)
            for k in range(nz)
        ]

    def step(self, i):
        if i == 0:
            self.own.start()
            self.p_own.start()
            self.s_own.start()
        elif i == 1:
            self.p_own.wait_recv()
            self.s_p.start()
        elif i == 2:
            self.own.wait()
            self.s_own.wait_recv()
            self.s_p.wait_recv()
            for t in self.zs:
                t.start()
            self.sibs[0].start()
        elif i == 3:
            for k, t in enumerate(self.zs):
                t.wait_recv()
                self.sibs[k + 1].start()
        else:
            super().step(i)


def add_blocks(count, dst, a, b):
    def body(i, _):
        dst(i)[...] = (a(i)[...].astype(f32) + b(i)[...].astype(f32)).astype(bf16)
        return 0

    lax.fori_loop(0, count, body, 0)


class Scatter:
    LOADS = (("core", 16), ("xy", 8), ("xy", 4), ("z", 8), None)
    WORK = (0.3, 1.2, 0.7, 0.4, 0.3)

    @staticmethod
    def shapes(nz, blk):
        return (nz, 2, 2, *blk), (2, nz, *blk), (nz, *blk), (nz - 1, *blk)

    @staticmethod
    def count(nz):
        return nz + 3

    def __init__(self, here, part, bufs, out, sems):
        self.h, self.out = here, out
        self.rc, self.rs, self.rp, self.rz = bufs
        h, nz = here, here.nz
        self.own = part.at[:, :, :, h.c]
        self.core = remote(part.at[:, :, :, 1 - h.c], self.rc, sems, 0, h.sib)
        self.s = [
            remote(self.rc.at[:, *h.column(p, 1 - h.s)], self.rs.at[p], sems, 1 + i, h.s_dev)
            for i, p in enumerate((1 - h.p, h.p))
        ]
        self.pp = remote(self.rs.at[1 - h.p], self.rp, sems, 3, h.p_dev)
        self.zs = [
            remote(self.rp.at[h.z_of[k]], self.rz.at[k - 1], sems, 3 + k, h.z_devs[k])
            for k in range(1, nz)
        ]

    def sum_core(self):
        at = lambda r: lambda i: r.at[lax.div(i, 4), lax.rem(lax.div(i, 2), 2), lax.rem(i, 2)]
        add_blocks(4 * self.h.nz, at(self.rc), at(self.rc), at(self.own))

    def step(self, i):
        h, nz = self.h, self.h.nz
        if i == 0:
            self.core.start()
        elif i == 1:
            self.core.wait_recv()
            self.sum_core()
            for t in self.s:
                t.start()
            self.core.wait_send()
        elif i == 2:
            for t in self.s:
                t.wait_recv()

            def kept(i):
                return self.rc.at[lax.rem(i, nz), *h.column(lax.div(i, nz), h.s)]

            mine = lambda i: self.rs.at[lax.div(i, nz), lax.rem(i, nz)]
            add_blocks(2 * nz, mine, mine, kept)
            self.pp.start()
        elif i == 3:
            self.pp.wait_recv()
            mine = lambda i: self.rp.at[i]
            add_blocks(nz, mine, mine, lambda i: self.rs.at[h.p, i])
            for t in self.zs:
                t.start()
        elif i == 4:
            for t in self.zs:
                t.wait_recv()
            total = self.rp[h.z].astype(f32)
            for k in range(nz - 1):
                total = total + self.rz[k].astype(f32)
            self.out[...] = total
        elif i == 5:
            for t in (*self.s, self.pp, *self.zs):
                t.wait_send()


class ScatterPlane(Scatter):
    LOADS = (("core", 16), ("z", 32), ("xy", 2), ("xy", 1), None)

    @staticmethod
    def shapes(nz, blk):
        return (nz, 2, 2, *blk), (nz - 1, 2, 2, *blk), (2, *blk), blk

    def __init__(self, here, part, bufs, out, sems):
        self.h, self.out = here, out
        self.rc, self.rz, self.rs, self.rp = bufs
        h, nz = here, here.nz
        self.own = part.at[:, :, :, h.c]
        self.core = remote(part.at[:, :, :, 1 - h.c], self.rc, sems, 0, h.sib)
        self.zs = [
            remote(self.rc.at[h.z_of[k]], self.rz.at[k - 1], sems, k, h.z_devs[k])
            for k in range(1, nz)
        ]
        self.s = [
            remote(self.rc.at[h.z, *h.column(p, 1 - h.s)], self.rs.at[p], sems, nz + p, h.s_dev)
            for p in range(2)
        ]
        self.pp = remote(self.rs.at[1 - h.p], self.rp, sems, nz + 2, h.p_dev)

    def step(self, i):
        h, nz = self.h, self.h.nz
        if i == 1:
            self.core.wait_recv()
            self.sum_core()
            for t in self.zs:
                t.start()
            self.core.wait_send()
        elif i == 2:
            for t in self.zs:
                t.wait_recv()

            def body(i, _):
                mine = self.rc.at[h.z, lax.div(i, 2), lax.rem(i, 2)]
                total = mine[...].astype(f32)
                for k in range(nz - 1):
                    total = total + self.rz[k, lax.div(i, 2), lax.rem(i, 2)].astype(f32)
                mine[...] = total.astype(bf16)
                return 0

            lax.fori_loop(0, 4, body, 0)
            for t in self.s:
                t.start()
        elif i == 3:
            for t in self.s:
                t.wait_recv()
            mine = lambda i: self.rs.at[i]
            add_blocks(2, mine, mine, lambda i: self.rc.at[h.z, *h.column(i, h.s)])
            self.pp.start()
        elif i == 4:
            self.pp.wait_recv()
            self.out[...] = self.rs[h.p].astype(f32) + self.rp[...].astype(f32)
        else:
            super().step(i)


class Planner:
    UNIT = {"xy": 0.8, "z": 0.8, "core": 0.1}
    HOP = 3.0

    def __init__(self, chunks, sizes):
        self.chunks, self.sizes = chunks, sizes
        self.now, self.free = 0.0, dict.fromkeys(self.UNIT, 0.0)
        self.ready, self.queue, self.arrived = {}, [], None
        self.held, self.ahead = [], 0

    def emit(self, i):
        step, when = self.ready.get(i, (0, 0.0))
        chunk, size = self.chunks[i], self.sizes[i]
        self.now = max(self.now, when) + chunk.WORK[step] * size
        chunk.step(step)
        load = chunk.LOADS[step]
        if load is None:
            del self.ready[i]
            if self.arrived:
                self.arrived(i)
            return
        if step == 1 and i + self.ahead in self.held:
            self.held.remove(i + self.ahead)
            self.emit(i + self.ahead)
        link, amount = load
        self.free[link] = max(self.free[link], self.now) + self.UNIT[link] * amount * size
        self.ready[i] = (step + 1, self.free[link] + self.HOP)

    def settle(self):
        while True:
            due = [(-s, i) for i, (s, when) in self.ready.items() if when <= self.now]
            if not due:
                return
            self.emit(min(due)[1])

    def free_slot(self, i):
        while i in self.ready and self.ready[i][0] == 1:
            self.emit(i)

    def compute(self, cost, work):
        self.settle()
        work()
        self.now += cost

    def later(self, cost, work):
        self.queue.append((cost, work))

    def finish(self):
        while self.ready or self.queue:
            self.settle()
            if self.queue:
                self.compute(*self.queue.pop(0))
            elif self.ready:
                self.emit(min(self.ready, key=lambda k: (self.ready[k][1], k)))
        for c in self.chunks:
            c.step(5)


def stats(v):
    mean = jnp.mean(v, axis=-1, keepdims=True)
    cen = v - mean
    r = lax.rsqrt(jnp.mean(cen * cen, axis=-1, keepdims=True) + EPS)
    return cen * r, r


def dot(a, b):
    return jnp.dot(a, b, preferred_element_type=f32)


def dot_nt(a, b):
    return lax.dot_general(a, b, (((1,), (1,)), ((), ())), preferred_element_type=f32)


def dot_tn(a, b):
    return lax.dot_general(a, b, (((0,), (0,)), ((), ())), preferred_element_type=f32)


def matrix(ref, lo=None, size=None):
    v = ref[...] if lo is None else ref[..., pl.ds(lo, size)]
    return v.reshape(-1, v.shape[-1])


def tiles(total, size, work):
    def body(i, _):
        work(pl.multiple_of(i * size, size))
        return 0

    lax.fori_loop(0, total // size, body, 0)


def span(start, size, unit=2 * HEAD):
    return pl.ds(pl.multiple_of(start, unit), size)


def head_lanes():
    lane = lax.broadcasted_iota(jnp.int32, (1, 2 * HEAD), 1)
    low = jnp.where(lane < HEAD, 1.0, 0.0)
    return low.astype(bf16), (1.0 - low).astype(bf16)


def softmax(s):
    e = jnp.exp(s - jnp.max(s, axis=-1, keepdims=True))
    return (e * (1.0 / jnp.sum(e, axis=-1, keepdims=True))).astype(bf16)


def pair(ref, rows, base, j):
    return ref.at[rows, pl.ds(pl.multiple_of(base + j * 2 * HEAD, 2 * HEAD), 2 * HEAD)]


SCALE = HEAD ** (-0.5)


def chunk_cols(weights, d):
    out = []
    for i, w in enumerate(weights):
        wide = d if w.shape[1] % d == 0 and i < 6 else d // 3
        out += [(i, s, wide) for s in range(0, w.shape[1], wide)]
    return out


def forward_kernel(nz, dims, chunks, *refs):
    b, t, d, kp, ff = dims
    n = len(chunks) + 1
    xs, mask, images, gsh = refs[:4]
    shards = refs[4:11]
    out = refs[11]
    res = refs[12 : 12 + N_RES]
    fulls = refs[12 + N_RES : 12 + N_RES + n]
    rest = refs[12 + N_RES + n :]
    (n1, qkv, p1, o1, x1, n2, q2, kv2, p2, o2, x2, n3, act, dg, grow, img) = keep = rest[:N_RES]
    g = rest[N_RES : N_RES + n]
    raw, mb, local, ssem, rsem, csem, isem = rest[N_RES + n :]
    here = Place(nz)
    seq = lax.axis_index("seq")
    patches = mask.shape[1]
    enter(here.partners())
    srcs = [gsh] + [shards[i].at[:, s : s + w] for i, s, w in chunks]
    gs = []
    for i in range(n):
        kind = GatherPlane if i in (11, 12) else Gather
        gs.append(kind(here, srcs[i], g[i], (ssem.at[i], rsem.at[i]), local.at[i]))
    sizes = [gsh.shape[-1] / d] + [r.shape[-1] * r.shape[-2] / (d * gsh.shape[0]) for r in g[1:]]
    plan = Planner(gs, sizes)
    plan.ahead = AHEAD
    plan.held = [i for i in range(AHEAD, n) if i not in (11, 12)]
    for i in range(n):
        if i not in plan.held:
            plan.emit(i)
    pictures = pltpu.make_async_copy(images.at[pl.ds(seq * b, b)], raw, isem.at[0])
    pictures.start()
    mb[...] = jnp.full(mb.shape, -1e30, f32)
    for i in range(b):
        row = mask[pl.ds(seq * b + i, 1), :]
        mb[i : i + 1, :patches] = jnp.where(row > 0, 0.0, -1e30)
    copies = []

    def flush(src, dst):
        cp = pltpu.make_async_copy(src, dst, csem.at[len(copies)])
        cp.start()
        copies.append(cp)

    def save(*which):
        for k in which:
            flush(keep[k], res[k])

    names = {}
    for k, (i, s, wide) in enumerate(chunks):
        names.setdefault(i, []).append(k + 1)
    lanes = head_lanes()
    heads = d // HEAD
    pairs = heads // 2
    tok = [slice(i * t, (i + 1) * t) for i in range(b)]
    pat = [slice(i * kp, (i + 1) * kp) for i in range(b)]

    def first():
        grow[...] = jnp.transpose(matrix(g[0]).astype(f32))[:8]

        def rows(r):
            h, _ = stats(xs[pl.ds(r, t)].astype(f32))
            n1[pl.ds(r, t)] = (h * grow[0:1]).astype(bf16)

        tiles(b * t, t, rows)
        save(0, 14)

    def project(src, k, dst, at):
        def tile(s):
            v = src()
            dst[:, span(at + s, 256)] = dot(v, matrix(g[k], s, 256)).astype(bf16)

        return lambda: tiles(g[k].shape[-1], 256, tile)

    def self_pairs(lo, hi):
        def body(j, _):
            causal = lax.broadcasted_iota(jnp.int32, (t, t), 0) >= lax.broadcasted_iota(
                jnp.int32, (t, t), 1
            )
            for i, r in enumerate(tok):
                q, k, v = (pair(qkv, r, m * d, j)[...] for m in range(3))
                o = jnp.zeros((t, 2 * HEAD), f32)
                for a in range(2):
                    s = dot_nt(q, k * lanes[a]) * SCALE
                    p = softmax(jnp.where(causal, s, -1e30))
                    p1[i * heads + 2 * j + a] = p
                    o = o + dot(p, v * lanes[a])
                pair(o1, r, 0, j)[...] = o.astype(bf16)
            return 0

        return lambda: lax.fori_loop(lo, hi, body, 0)

    def cross_pairs(lo, hi):
        def body(j, _):
            for i, r in enumerate(tok):
                q = pair(q2, r, 0, j)[...]
                k, v = (pair(kv2, pat[i], m * d, j)[...] for m in range(2))
                bias = mb[i : i + 1]
                o = jnp.zeros((t, 2 * HEAD), f32)
                for a in range(2):
                    p = softmax(dot_nt(q, k * lanes[a]) * SCALE + bias)
                    p2[i * heads + 2 * j + a] = p
                    o = o + dot(p, v * lanes[a])
                pair(o2, r, 0, j)[...] = o.astype(bf16)
            return 0

        return lambda: lax.fori_loop(lo, hi, body, 0)

    def residual(base, o, k, dst, row, normed):
        def rows(s):
            r = pl.ds(s, t)
            v = base[r].astype(f32) + dot(o[r], matrix(g[k]))
            dst[r] = v
            h, _ = stats(v)
            normed[r] = (h * grow[row : row + 1]).astype(bf16)

        return lambda: tiles(b * t, t, rows)

    def mlp_up(k, at):
        def tile(s):
            h = dot(n3[...], matrix(g[k], s, 256))
            cols = span(at + s, 256)
            cdf = 0.5 * (1.0 + lax.erf(h * (0.5**0.5)))
            act[:, cols] = (h * cdf).astype(bf16)
            pdf = jnp.exp(-0.5 * h * h) * (0.5 / jnp.pi) ** 0.5
            dg[:, cols] = (cdf + h * pdf).astype(bf16)

        return lambda: tiles(g[k].shape[-1], 256, tile)

    def mlp_down(k, at):
        wide = g[k].shape[-1]

        def rows(s):
            r = pl.ds(s, t)
            y = x2[r, at : at + wide] + dot(act[r], matrix(g[k]))
            out[r, at : at + wide] = y.astype(bf16)

        return lambda: tiles(b * t, t, rows)

    def images_here():
        pictures.wait()
        whole = patches // 16 * 16
        for i in range(b):
            img[i * kp : i * kp + whole] = raw[i, :whole]
            if whole < patches:
                img[i * kp + whole : (i + 1) * kp] = jnp.zeros((kp - whole, d), bf16)
                img[i * kp + whole : i * kp + patches] = raw[i, whole:]
        save(15)

    third = [(i * pairs // 3, (i + 1) * pairs // 3) for i in range(3)]

    landed = set()

    def arrived(c):
        flush(g[c], fulls[c])
        landed.add(c)
        while queued[0] in landed:
            use(queued[0])
            queued[0] += 1

    queued = [0]

    def use(c):
        add = plan.later
        if c == 0:
            add(2.0, first)
            add(0.0, images_here)
            return
        i, s, wide = chunks[c - 1]
        last = c == names[i][-1]
        if i == 0:
            add(1.7, project(lambda: n1[...], c, qkv, s))
            if last:
                add(0.0, lambda: save(1))
                for lo, hi in third:
                    add(2.5, self_pairs(lo, hi))
                add(0.0, lambda: save(2, 3))
        elif i == 1:
            add(2.5, residual(xs, o1, c, x1, 1, n2))
            add(0.0, lambda: save(4, 5))
        elif i == 2:
            add(1.7, project(lambda: n2[...], c, q2, 0))
            add(0.0, lambda: save(6))
        elif i == 3:
            add(2.5, project(lambda: img[...], c, kv2, s))
            if last:
                add(0.0, lambda: save(7))
                for lo, hi in third:
                    add(3.0, cross_pairs(lo, hi))
                add(0.0, lambda: save(8, 9))
        elif i == 4:
            add(2.5, residual(x1, o2, c, x2, 2, n3))
            add(0.0, lambda: save(10, 11))
        elif i == 5:
            add(3.5, mlp_up(c, s))
            if last:
                add(0.0, lambda: save(12, 13))
        else:
            add(2.0, mlp_down(c, s))

    plan.arrived = arrived
    plan.finish()
    for cp in copies:
        cp.wait()


N_RES = 16
AHEAD = 99


def residual_shapes(b, t, d, kp, ff):
    m, heads = b * t, d // HEAD
    S = jax.ShapeDtypeStruct
    tok, tokf = S((m, d), bf16), S((m, d), f32)
    return [
        tok, S((m, 3 * d), bf16), S((b * heads, t, t), bf16), tok, tokf, tok, tok,
        S((b * kp, 2 * d), bf16), S((b * heads, t, kp), bf16), tok, tokf, tok,
        S((m, ff), bf16), S((m, ff), bf16), S((8, d), f32), S((b * kp, d), bf16),
    ]


def forward(nz, xs, images, mask, gains, weights):
    b, t, d = xs.shape
    kp, ff = padded(images.shape[1]), weights[5].shape[1]
    chunks = chunk_cols(weights, d)
    n = len(chunks) + 1
    res = residual_shapes(b, t, d, kp, ff)
    blocks = [gains.shape] + [(weights[i].shape[0], w) for i, _, w in chunks]
    fulls = [jax.ShapeDtypeStruct((nz, 2, 2, 2, *s), bf16) for s in blocks]
    count = Gather.count(nz)
    hbm, vm = pl.BlockSpec(memory_space=HBM), pl.BlockSpec(memory_space=VMEM)
    outs = pl.pallas_call(
        functools.partial(forward_kernel, nz, (b, t, d, kp, ff), chunks),
        out_shape=[jax.ShapeDtypeStruct((b * t, d), bf16), *res, *fulls],
        in_specs=[vm, vm, *([hbm] * 9)],
        out_specs=[vm, *([hbm] * (N_RES + n))],
        scratch_shapes=[
            *(pltpu.VMEM(s.shape, s.dtype) for s in (*res, *fulls)),
            pltpu.VMEM((b, *images.shape[1:]), bf16),
            pltpu.VMEM((b + -b % 8, kp), f32),
            pltpu.SemaphoreType.DMA((n,)),
            pltpu.SemaphoreType.DMA((n, count)),
            pltpu.SemaphoreType.DMA((n, count)),
            pltpu.SemaphoreType.DMA((N_RES + n,)),
            pltpu.SemaphoreType.DMA((1,)),
        ],
        compiler_params=pltpu.CompilerParams(
            collective_id=0, has_side_effects=True, vmem_limit_bytes=60 << 20
        ),
    )(xs.reshape(b * t, d), mask, images, gains, *weights)
    return outs[0], outs[1 : 1 + N_RES], outs[1 + N_RES :]


def padded(patches):
    return patches + -patches % 16


def backward_kernel(nz, dims, chunks, *refs):
    b, t, d, kp, ff = dims
    heads = d // HEAD
    pairs = heads // 2
    m = b * t
    n_c = len(chunks)
    order = [*range(n_c - 3, n_c), *range(n_c - 7, n_c - 3), 7, 5, 6, 4, 3, None, 0, 1, 2]
    n = len(order)
    h_in = refs[: 2 + N_RES + n_c]
    h_cot, h_xs = h_in[:2]
    res = dict(zip(RES_NAMES, h_in[2 : 2 + N_RES]))
    full = h_in[2 + N_RES :]
    at = len(h_in)
    gx_out, img_out = refs[at : at + 2]
    outs = refs[at + 2 : at + 9]
    gg_out = refs[at + 9]
    rest = list(refs[at + 10 :])
    take = lambda k: [rest.pop(0) for _ in range(k)]
    cot, act, dg, n3, xf, o2, p2, q2, kv2, img, n2, o1, p1, n1, xs, grow = take(16)
    gx, gxb, go, gi, ggr = take(5)
    wd, ws = take(3), take(6)
    pd, ps, pg = take(3), take(4), take(1)[0]
    bufs = [take(4) for _ in range(n)]
    lsem, ssem, rsem, isem, jsem, osem = rest
    here, broad = Place(nz), Place(nz, wide=True)
    dp, seq = lax.axis_index("dp"), lax.axis_index("seq")
    peers = [(dp, lax.rem(seq + k, 4)) for k in range(1, 4)]

    loads, waits = {}, {}

    def load(name, src, dst):
        cp = pltpu.make_async_copy(src, dst, lsem.at[len(loads)])
        loads[name] = cp
        cp.start()

    def need(*names):
        for k in names:
            if k in loads and k not in waits:
                loads[k].wait()
                waits[k] = True

    q_at = act.at[:, : 3 * d]
    load("act", res["act"], act)
    load("cot", h_cot, cot)
    for j in range(3):
        load("wd%d" % j, full[n_c - 3 + j], wd[j])
    load("dg", res["dg"], dg)
    load("n3", res["n3"], n3)
    for j in range(4):
        load("up%d" % j, full[n_c - 7 + j], ws[j])
    load("x2", res["x2"], xf)
    load("grow", res["grow"], grow)
    for name, dst in (("o2", o2), ("p2", p2), ("q2", q2), ("kv2", kv2)):
        load(name, res[name], dst)
    load("img", res["img"], img)
    load("co", full[7], ws[4])
    load("ckv0", full[5], ws[5])
    for name, dst in (("n2", n2), ("o1", o1), ("p1", p1), ("n1", n1)):
        load(name, res[name], dst)
    load("xs", h_xs, xs)
    enter([*here.partners(), *peers])
    ggr[...] = jnp.zeros_like(ggr)

    parts, small = [], 0
    for k in order:
        if k is None:
            parts.append(pg)
        elif k >= n_c - 3:
            parts.append(pd[k - (n_c - 3)])
        else:
            parts.append(ps[small % 4])
            small += 1
    place = {k: i for i, k in enumerate(order)}
    dst = [
        gg_out if k is None else outs[chunks[k][0]].at[:, chunks[k][1] : chunks[k][1] + chunks[k][2]]
        for k in order
    ]
    sc = []
    for i in range(n):
        kind = ScatterPlane if i in PLANES else Scatter
        at = broad if i in BROAD else here
        sc.append(kind(at, parts[i], bufs[i], dst[i], (ssem.at[i], rsem.at[i])))
    sizes = [0.2 if k is None else 1.35 if k >= n_c - 3 else 1.0 for k in order]
    plan = Planner(sc, sizes)
    smalls = [i for i, k in enumerate(order) if k is not None and k < n_c - 3]

    def slot_ready(i):
        if i in smalls and smalls.index(i) >= 4:
            plan.free_slot(smalls[smalls.index(i) - 4])

    lanes = head_lanes()
    tok = [slice(i * t, (i + 1) * t) for i in range(b)]
    pat = [slice(i * kp, (i + 1) * kp) for i in range(b)]

    def grad_small(k, x, dy, first, cost):
        i = place[k]
        slot_ready(i)

        def work():
            rows = x()
            for s in range(0, d, 256):
                r = dot_tn(rows, dy[:, first + s : first + s + 256])
                parts[i][:, :, :, :, :, s : s + 256] = r.reshape(nz, 2, 2, 2, -1, 256).astype(bf16)

        plan.compute(cost, work)
        plan.emit(i)

    def grad_down(j):
        k = n_c - 3 + j
        i = place[k]
        wide = d // 3

        rows = ff // nz

        def work(z, _):
            r = dot_tn(act[:, span(z * rows, rows)], cot[:, j * wide : (j + 1) * wide])
            parts[i][z] = r.reshape(2, 2, 2, -1, wide).astype(bf16)
            return 0

        plan.compute(1.8, lambda: lax.fori_loop(0, nz, work, 0))
        plan.emit(i)

    def hidden(z):
        half, wide = ff // nz // 2, d // 3

        def work(x, _):
            g = None
            for j in range(3):
                w = wd[j][z, x].reshape(half, wide)
                term = dot_nt(cot[:, j * wide : (j + 1) * wide], w)
                g = term if g is None else g + term
            at = span((2 * z + x) * half, half)
            dg[:, at] = (g * dg[:, at].astype(f32)).astype(bf16)
            return 0

        plan.compute(1.3, lambda: lax.fori_loop(0, 2, work, 0))

    def norm_grad(src, ups, base, row, first):
        ggr[row : row + 1] = jnp.zeros((1, d), f32)

        def work(s):
            r = pl.ds(s, t)
            e = None
            for j, w in enumerate(ups):
                term = dot_nt(src[r, j * d : (j + 1) * d], matrix(w))
                e = term if e is None else e + term
            h, rs = stats(base[r].astype(f32))
            u = e * grow[row : row + 1]
            mu = jnp.mean(u, axis=-1, keepdims=True)
            mx = jnp.mean(u * h, axis=-1, keepdims=True)
            prev = cot[r].astype(f32) if first else gx[r]
            v = prev + rs * (u - mu - h * mx)
            gx[r] = v
            gxb[r] = v.astype(bf16)
            ggr[row : row + 1] += jnp.sum(e * h, axis=0, keepdims=True)

        plan.compute(1.5 + 1.2 * len(ups), lambda: tiles(m, t, work))

    def back_project(w):
        half = d // 2

        def work(s, _):
            rows = w[pl.ds(s * (nz // 2), nz // 2)].reshape(half, d)
            go[:, span(s * half, half)] = dot_nt(gxb[...], rows).astype(bf16)
            return 0

        plan.compute(1.4, lambda: lax.fori_loop(0, 2, work, 0))

    def pairs_back(lo, hi, p_ref, q_ref, q_base, kv_ref, kv_base, rows):
        def body(j, _):
            for i, r in enumerate(tok):
                rk = rows[i]
                q, g = pair(q_ref, r, q_base, j)[...], pair(go, r, 0, j)[...]
                k, v = (pair(kv_ref, rk, kv_base + x * d, j)[...] for x in range(2))
                dq = dk = dv = None
                for a in range(2):
                    lane = lanes[a]
                    pb = p_ref[i * heads + 2 * j + a]
                    p = pb.astype(f32)
                    dpr = dot_nt(g, v * lane)
                    pd = dpr * p
                    ds = ((pd - p * jnp.sum(pd, axis=-1, keepdims=True)) * SCALE).astype(bf16)
                    terms = (dot(ds, k * lane), dot_tn(ds, q * lane), dot_tn(pb, g * lane))
                    if a == 0:
                        dq, dk, dv = terms
                    else:
                        dq, dk, dv = dq + terms[0], dk + terms[1], dv + terms[2]
                pair(q_ref, r, q_base, j)[...] = dq.astype(bf16)
                pair(kv_ref, rk, kv_base, j)[...] = dk.astype(bf16)
                pair(kv_ref, rk, kv_base + d, j)[...] = dv.astype(bf16)
            return 0

        return lambda: lax.fori_loop(lo, hi, body, 0)

    thirds = [(i * pairs // 3, (i + 1) * pairs // 3) for i in range(3)]

    need("act", "cot")
    for j in range(3):
        grad_down(j)
    load("qkv", res["qkv"], q_at)
    need("wd0", "wd1", "wd2", "dg")
    for z in range(nz):
        hidden(z)
    need("n3")
    for j in range(4):
        grad_small(n_c - 7 + j, lambda: n3[...], dg, j * d, 1.4)
    need("up0", "up1", "up2", "up3", "x2", "grow")
    norm_grad(dg, ws[:4], xf, 2, True)
    load("x1", res["x1"], xf)
    load("ckv1", full[6], ws[0])
    load("cq", full[4], ws[1])
    load("so", full[3], ws[2])
    load("qkv0", full[0], ws[3])
    need("co")
    back_project(ws[4])
    load("qkv1", full[1], ws[4])
    need("o2")
    grad_small(7, lambda: o2[...], gxb, 0, 1.4)
    need("p2", "q2", "kv2")
    for lo, hi in thirds:
        plan.compute(4.0, pairs_back(lo, hi, p2, q2, 0, kv2, 0, pat))
    need("img")
    grad_small(5, lambda: img[...], kv2, 0, 2.0)
    grad_small(6, lambda: img[...], kv2, d, 2.0)
    need("ckv0", "ckv1")
    wide = d // 4

    def image_grad(i, _):
        r = span(i * kp, kp, 16)
        y = dot_nt(matrix(ws[5]), kv2[r, :d]) + dot_nt(matrix(ws[0]), kv2[r, d:])
        y = y.astype(bf16)
        for s in range(4):
            gi[s, i] = y[s * wide : (s + 1) * wide]
        return 0

    plan.compute(4.0, lambda: lax.fori_loop(0, b, image_grad, 0))
    keep = pltpu.make_async_copy(gi.at[seq], img_out.at[seq], osem.at[0])
    keep.start()
    moves = [
        remote(gi.at[lax.rem(seq + k, 4)], img_out.at[seq], (isem, jsem), k - 1, peers[k - 1])
        for k in range(1, 4)
    ]
    for mv in moves:
        mv.start()
    load("qkv2", full[2], ws[5])
    need("n2", "cq", "x1")
    norm_grad(q2, [ws[1]], xf, 1, False)
    need("so")
    back_project(ws[2])
    grad_small(4, lambda: n2[...], q2, 0, 1.4)
    need("o1")
    grad_small(3, lambda: o1[...], gxb, 0, 1.4)
    need("p1", "qkv")
    for lo, hi in thirds:
        plan.compute(3.0, pairs_back(lo, hi, p1, act, 0, act, d, tok))
    need("xs", "qkv0", "qkv1", "qkv2", "n1")
    norm_grad(act, [ws[3], ws[4], ws[5]], xs, 0, False)
    gx_copy = pltpu.make_async_copy(gx, gx_out, osem.at[1])
    gx_copy.start()

    def gain_terms():
        r = jnp.transpose(ggr[...])
        pg[...] = r.reshape(nz, 2, 2, 2, -1, LANES).astype(bf16)

    plan.compute(0.7, gain_terms)
    plan.emit(place[None])
    for j in range(3):
        grad_small(j, lambda: n1[...], act, j * d, 1.4)
    plan.finish()
    keep.wait()
    gx_copy.wait()
    for mv in moves:
        mv.wait()


PLANES = (0, 3)
BROAD = ()

RES_NAMES = (
    "n1", "qkv", "p1", "o1", "x1", "n2", "q2", "kv2",
    "p2", "o2", "x2", "n3", "act", "dg", "grow", "img",
)


def backward(nz, cot, patches, xs, weights, res, fulls):
    b, t, d = xs.shape
    kp, ff = padded(patches), weights[5].shape[1]
    m, heads = b * t, d // HEAD
    chunks = chunk_cols(weights, d)
    n_c = len(chunks)
    n = n_c + 1
    rows = weights[0].shape[0]
    down = (weights[6].shape[0], d // 3)
    tok, tokf = pltpu.VMEM((m, d), bf16), pltpu.VMEM((m, d), f32)
    part = lambda blk: pltpu.VMEM((nz, 2, 2, 2, *blk), bf16)
    blocks = [down] * 3 + [(rows, d)] * 9 + [(rows, LANES)] + [(rows, d)] * 3
    bufs = []
    for i, blk in enumerate(blocks):
        kind = ScatterPlane if i in PLANES else Scatter
        bufs += [pltpu.VMEM(s, bf16) for s in kind.shapes(nz, blk)]
    count = Scatter.count(nz)
    hbm, vm = pl.BlockSpec(memory_space=HBM), pl.BlockSpec(memory_space=VMEM)
    hid = pltpu.VMEM((m, ff), bf16)
    S = jax.ShapeDtypeStruct
    outs = pl.pallas_call(
        functools.partial(backward_kernel, nz, (b, t, d, kp, ff), chunks),
        out_shape=[
            S((m, d), f32), S((4, b, d // 4, kp), bf16),
            *(S(w.shape, f32) for w in weights), S((rows, LANES), f32),
        ],
        in_specs=[hbm] * (2 + N_RES + n_c),
        out_specs=[hbm, hbm, *([vm] * 8)],
        scratch_shapes=[
            tok, hid, hid, tok, tokf, tok, pltpu.VMEM((b * heads, t, kp), bf16), tok,
            pltpu.VMEM((b * kp, 2 * d), bf16), pltpu.VMEM((b * kp, d), bf16), tok, tok,
            pltpu.VMEM((b * heads, t, t), bf16), tok, tok, pltpu.VMEM((8, d), f32),
            tokf, tok, tok, pltpu.VMEM((4, b, d // 4, kp), bf16), pltpu.VMEM((LANES, d), f32),
            *([part(down)] * 3), *([part((rows, d))] * 6),
            *([part(down)] * 3), *([part((rows, d))] * 4), part((rows, LANES)),
            *bufs,
            pltpu.SemaphoreType.DMA((2 + N_RES + n_c,)),
            pltpu.SemaphoreType.DMA((n, count)),
            pltpu.SemaphoreType.DMA((n, count)),
            pltpu.SemaphoreType.DMA((3,)),
            pltpu.SemaphoreType.DMA((3,)),
            pltpu.SemaphoreType.DMA((2,)),
        ],
        compiler_params=pltpu.CompilerParams(
            collective_id=1, has_side_effects=True, vmem_limit_bytes=63 << 20
        ),
    )(cot.reshape(m, d), xs.reshape(m, d), *res, *fulls)
    return outs


def finish_kernel(n, *refs):
    ins, gi, gg = refs[:n], refs[n], refs[n + 1]
    outs, go, gains = refs[n + 2 : 2 * n + 2], refs[2 * n + 2], refs[2 * n + 3 : 2 * n + 6]
    held, pics, wide = refs[2 * n + 6 : 3 * n + 6], refs[3 * n + 6], refs[3 * n + 7]
    isem, osem = refs[3 * n + 8 :]
    arrive = [pltpu.make_async_copy(ins[i], held[i], isem.at[i]) for i in range(n)]
    leave = [pltpu.make_async_copy(held[i], outs[i], osem.at[i]) for i in range(n)]
    half = gi.shape[0] // 2
    parts = [pl.ds(k * half, half) for k in range(2)]
    p_in = [pltpu.make_async_copy(gi.at[r], pics.at[r], isem.at[n + k]) for k, r in enumerate(parts)]
    p_out = [pltpu.make_async_copy(wide.at[r], go.at[r], osem.at[n + k]) for k, r in enumerate(parts)]
    for cp in (*p_in, *arrive):
        cp.start()

    def widen(i, _):
        wide[i] = pics[i].astype(f32)[:, : wide.shape[2]]
        return 0

    for k in range(2):
        p_in[k].wait()
        lax.fori_loop(k * half, (k + 1) * half, widen, 0)
        p_out[k].start()
    for i in range(n):
        arrive[i].wait()
        leave[i].start()
    row = jnp.transpose(gg[...])
    for k, r in enumerate(gains):
        r[...] = row[k, : r.shape[0]]
    for cp in (*p_out, *leave):
        cp.wait()


def finish(arrays, gi, gg, patches):
    n = len(arrays)
    hbm, vm = pl.BlockSpec(memory_space=HBM), pl.BlockSpec(memory_space=VMEM)
    S = jax.ShapeDtypeStruct
    vec = S((gg.shape[0],), f32)
    return pl.pallas_call(
        functools.partial(finish_kernel, n),
        out_shape=[
            *(S(a.shape, a.dtype) for a in arrays), S((*gi.shape[:2], patches), f32), vec, vec, vec
        ],
        in_specs=[*([hbm] * (n + 1)), vm],
        out_specs=[*([hbm] * (n + 1)), vm, vm, vm],
        scratch_shapes=[
            *(pltpu.VMEM(a.shape, a.dtype) for a in arrays),
            pltpu.VMEM(gi.shape, bf16), pltpu.VMEM((*gi.shape[:2], patches), f32),
            pltpu.SemaphoreType.DMA((n + 2,)), pltpu.SemaphoreType.DMA((n + 2,)),
        ],
        compiler_params=pltpu.CompilerParams(vmem_limit_bytes=62 << 20),
    )(*arrays, gi, gg)


def norm_stats(v):
    mean = jnp.mean(v, axis=-1, keepdims=True)
    centered = v - mean
    r = lax.rsqrt(jnp.mean(centered * centered, axis=-1, keepdims=True) + EPS)
    return centered * r, r


def norm_back(xhat, r, gain, e):
    u = e * gain
    mu = jnp.mean(u, axis=-1, keepdims=True)
    mx = jnp.mean(u * xhat, axis=-1, keepdims=True)
    return r * (u - mu - xhat * mx), jnp.sum(e * xhat, axis=(0, 1))


def mm(a, b):
    return jnp.einsum("btd,de->bte", a, b, preferred_element_type=f32)


def mm_t(a, b):
    return jnp.einsum("bte,de->btd", a, b, preferred_element_type=f32)


def wgrad(a, b):
    return jnp.einsum("btd,bte->de", a, b, preferred_element_type=f32)


def split_heads(a):
    b, t, _ = a.shape
    return a.reshape(b, t, -1, HEAD)


def attend(q, k, v, allowed):
    s = jnp.einsum("bqhe,bkhe->bhqk", q, k, preferred_element_type=f32) * HEAD ** (-0.5)
    s = jnp.where(allowed, s, -1e30)
    ex = jnp.exp(s - jnp.max(s, axis=-1, keepdims=True))
    p = ex / jnp.sum(ex, axis=-1, keepdims=True)
    o = jnp.einsum("bhqk,bkhe->bqhe", p.astype(bf16), v, preferred_element_type=f32)
    return p, o.astype(bf16)


def attend_back(q, k, v, p, g):
    dp = jnp.einsum("bqhe,bkhe->bhqk", g, v, preferred_element_type=f32)
    ds = (p * (dp - jnp.sum(dp * p, axis=-1, keepdims=True)) * HEAD ** (-0.5)).astype(bf16)
    dq = jnp.einsum("bhqk,bkhe->bqhe", ds, k, preferred_element_type=f32).astype(bf16)
    dk = jnp.einsum("bhqk,bqhe->bkhe", ds, q, preferred_element_type=f32).astype(bf16)
    dv = jnp.einsum("bhqk,bqhe->bkhe", p.astype(bf16), g, preferred_element_type=f32).astype(bf16)
    return dq, dk, dv


def layer(x0, img, mask, gains, weights, cot):
    g1, g2, g3 = (g.astype(f32) for g in gains)
    w_qkv, w_so, w_cq, w_ckv, w_co, w_up, w_down = weights
    b, t, d = x0.shape
    x = x0.astype(f32)
    pos = jnp.arange(t)
    causal = (pos[:, None] >= pos[None, :])[None, None]
    allowed = (mask > 0)[:, None, None, :]
    h1, r1 = norm_stats(x)
    n1 = (h1 * g1).astype(bf16)
    qkv = mm(n1, w_qkv).astype(bf16)
    q1, k1, v1 = (split_heads(qkv[..., i * d : (i + 1) * d]) for i in range(3))
    p1, o1 = attend(q1, k1, v1, causal)
    o1 = o1.reshape(b, t, d)
    x1 = x + mm(o1, w_so)
    h2, r2 = norm_stats(x1)
    n2 = (h2 * g2).astype(bf16)
    q2 = split_heads(mm(n2, w_cq).astype(bf16))
    kv = mm(img, w_ckv).astype(bf16)
    k2, v2 = split_heads(kv[..., :d]), split_heads(kv[..., d:])
    p2, o2 = attend(q2, k2, v2, allowed)
    o2 = o2.reshape(b, t, d)
    x2 = x1 + mm(o2, w_co)
    h3, r3 = norm_stats(x2)
    n3 = (h3 * g3).astype(bf16)
    hpre = mm(n3, w_up)
    cdf = 0.5 * (1.0 + lax.erf(hpre * (0.5**0.5)))
    act = (hpre * cdf).astype(bf16)
    out = (x2 + mm(act, w_down)).astype(bf16)

    gw_down = wgrad(act, cot)
    pdf = jnp.exp(-0.5 * hpre * hpre) * (0.5 / jnp.pi) ** 0.5
    gh = (mm_t(cot, w_down) * (cdf + hpre * pdf)).astype(bf16)
    gw_up = wgrad(n3, gh)
    dx2, gg3 = norm_back(h3, r3, g3, mm_t(gh, w_up))
    gx2 = cot.astype(f32) + dx2
    gx2b = gx2.astype(bf16)
    gw_co = wgrad(o2, gx2b)
    go2 = split_heads(mm_t(gx2b, w_co).astype(bf16))
    dq2, dk2, dv2 = attend_back(q2, k2, v2, p2, go2)
    dq2 = dq2.reshape(b, t, d)
    dkv = jnp.concatenate([dk2.reshape(b, -1, d), dv2.reshape(b, -1, d)], axis=-1)
    gw_ckv = wgrad(img, dkv)
    gimg = mm_t(dkv, w_ckv).astype(bf16)
    gw_cq = wgrad(n2, dq2)
    dx1, gg2 = norm_back(h2, r2, g2, mm_t(dq2, w_cq))
    gx1 = gx2 + dx1
    gx1b = gx1.astype(bf16)
    gw_so = wgrad(o1, gx1b)
    go1 = split_heads(mm_t(gx1b, w_so).astype(bf16))
    dq1, dk1, dv1 = attend_back(q1, k1, v1, p1, go1)
    dqkv = jnp.concatenate([a.reshape(b, t, d) for a in (dq1, dk1, dv1)], axis=-1)
    gw_qkv = wgrad(n1, dqkv)
    dx0, gg1 = norm_back(h1, r1, g1, mm_t(dqkv, w_qkv))
    gx0 = gx1 + dx0
    return out, gx0, gimg, (gg1, gg2, gg3), (gw_qkv, gw_so, gw_cq, gw_ckv, gw_co, gw_up, gw_down)


def native(captions, img, mask, gains, weights, cotangent):
    full = [lax.all_gather(w, BOTH, axis=0, tiled=True) for w in weights]
    gains = lax.all_gather(gains, BOTH, axis=0, tiled=True)
    gains = tuple(gains[:, i] for i in range(3))
    out, gx0, gimg, gg, gw = layer(captions, img, mask, gains, full, cotangent)
    gg = lax.psum_scatter(jnp.stack(gg, axis=1), BOTH, scatter_dimension=0, tiled=True)
    shards = [
        lax.psum_scatter(g.astype(bf16), BOTH, scatter_dimension=0, tiled=True).astype(f32)
        for g in gw
    ]
    gimg = lax.all_to_all(gimg, "seq", split_axis=2, concat_axis=0, tiled=True)
    return (out, gx0, gimg.astype(f32), gg[:, 0], gg[:, 1], gg[:, 2], *shards)


def on_device(captions, images, tissue_mask, gain_self, gain_cross, gain_mlp, *rest):
    weights, cotangent = rest[:-1], rest[-1]
    n_dp, n_seq = lax.axis_size("dp"), lax.axis_size("seq")
    b, t, d = captions.shape
    patches = images.shape[1]
    if n_seq != 4 or n_dp % 4 or any(w.shape[0] % 8 for w in weights):
        start = lax.axis_index("seq") * b
        img = lax.dynamic_slice_in_dim(images, start, b, 0)
        mask = lax.dynamic_slice_in_dim(tissue_mask, start, b, 0)
        gains = jnp.stack([gain_self, gain_cross, gain_mlp], axis=1)
        return native(captions, img, mask, gains, weights, cotangent)
    nz = n_dp // 2
    lane = lax.broadcasted_iota(jnp.int32, (gain_self.shape[0], LANES), 1)
    gains = jnp.zeros(lane.shape, bf16)
    for i, gain in enumerate((gain_self, gain_cross, gain_mlp)):
        gains = jnp.where(lane == i, gain[:, None], gains)
    out, res, fulls = forward(nz, captions, images, tissue_mask, gains, weights)
    gx, gimg, *gw, gg = backward(nz, cotangent, patches, captions, weights, res, fulls[1:])
    gimg = gimg.reshape(4 * b, *gimg.shape[2:])
    out, gx, *gw, gimg, gs, gc, gm = finish([out, gx, *gw], gimg, gg, patches)
    out, gx = out.reshape(b, t, d), gx.reshape(b, t, d)
    return (out, gx, gimg.swapaxes(1, 2), gs, gc, gm, *gw)


def solution(mesh):
    tok = P(BOTH, None, None)
    vec = P(BOTH)
    mat = P(BOTH, None)
    return jax.shard_map(
        on_device,
        mesh=mesh,
        in_specs=(tok, P("dp", None, None), P("dp", None), vec, vec, vec, *([mat] * 7), tok),
        out_specs=(tok, tok, P("dp", None, "seq"), vec, vec, vec, *([mat] * 7)),
        check_vma=False,
    )
```

profile of v0, /device:TPU:0, one launch (start us, length us, event | category | flops | bytes accessed | tf_op | source)
XLA Modules:
  0.0 219.4 jit_solution(2715271178552994197)
XLA Ops:
  0.7 1.4 select_select_fusion.refs_3_
  2.0 98.6 %shard_map.237 = (bf16[384,768]{1,0:T(8,128)(2,1)}, bf16[384,768]{1,0:T(8,128)(2,1)}, bf16[384,2304]{1,0:T(8,128)(2,1)}, bf16[36,128,128]{2,1,0:T(8,128)(2,1)}, ...) custom-call(bf16[384,768]{1,0:T(8,128)(2,1)} %bitcast.6, ...), custom_call_target="tpu_custom_call" | custom-call | tf_op jit(solution)/shard_map/pallas_call | solution.py:654
  100.7 113.6 %shard_map.238 = (f32[384,768]{1,0:T(8,128)}, bf16[4,3,192,208]{3,2,1,0:T(8,128)(2,1)}, f32[24,2304]{1,0:T(8,128)}, f32[24,768]{1,0:T(8,128)}, f32[24,768]{1,0:T...) custom-call(bf16[384,768]{1,0:T(8,128)(2,1)} %bitcast.9, ...), custom_call_target="tpu_custom_call" | custom-call | tf_op jit(solution)/shard_map/pallas_call | solution.py:984
  214.3 4.9 %shard_map.239 = (bf16[384,768]{1,0:T(8,128)(2,1)}, f32[384,768]{1,0:T(8,128)}, f32[24,2304]{1,0:T(8,128)}, f32[24,768]{1,0:T(8,128)}, f32[24,768]{1,0:T(8,128)}...) custom-call(bf16[384,768]{1,0:T(8,128)(2,1)} %get-tuple-element.68.r, ...), custom_call_target="tpu_custom_call" | custom-call | tf_op jit(solution)/shard_map/pallas_call | solution.py:1051
  (2 shorter events, 0.0 us)
where the time goes:
time: 220 us; the launch traced here: 219 us
  Pallas kernels  217 us (99%)
    pallas_call x1, Pallas kernels, backward(): pl.pallas_call(functools.partial(backward_kernel, nz, (b, t, d, kp, ff),...  114 us
    pallas_call x1, Pallas kernels, forward(): pl.pallas_call(functools.partial(forward_kernel, nz, (b, t, d, kp, ff), c...  98.6 us
    pallas_call x1, Pallas kernels, finish(): pl.pallas_call(functools.partial(finish_kernel, n), out_shape=[*(S(a.shap...  4.93 us

commit v1 on v0

--- a/solution.py
+++ b/solution.py
@@ -426,18 +426,25 @@
 def forward_kernel(nz, dims, chunks, *refs):
     b, t, d, kp, ff = dims
     n = len(chunks) + 1
-    xs, mask, images, gsh = refs[:4]
-    shards = refs[4:11]
-    out = refs[11]
-    res = refs[12 : 12 + N_RES]
-    fulls = refs[12 + N_RES : 12 + N_RES + n]
-    rest = refs[12 + N_RES + n :]
+    xs, mask = refs[:2]
+    gains = refs[2:5]
+    images = refs[5]
+    shards = refs[6:13]
+    out = refs[13]
+    res = refs[14 : 14 + N_RES]
+    fulls = refs[14 + N_RES : 14 + N_RES + n]
+    rest = refs[14 + N_RES + n :]
     (n1, qkv, p1, o1, x1, n2, q2, kv2, p2, o2, x2, n3, act, dg, grow, img) = keep = rest[:N_RES]
     g = rest[N_RES : N_RES + n]
-    raw, mb, local, ssem, rsem, csem, isem = rest[N_RES + n :]
+    raw, mb, gsh, turn, local, ssem, rsem, csem, isem = rest[N_RES + n :]
     here = Place(nz)
     seq = lax.axis_index("seq")
     patches = mask.shape[1]
+    turn[...] = jnp.zeros(turn.shape, f32)
+    for i, gain in enumerate(gains):
+        turn[i : i + 1, : gain.shape[0]] = gain[...].astype(f32).reshape(1, -1)
+    gsh[...] = jnp.zeros(gsh.shape, bf16)
+    gsh[:, :8] = jnp.transpose(turn[...])[: gsh.shape[0]].astype(bf16)
     enter(here.partners())
     srcs = [gsh] + [shards[i].at[:, s : s + w] for i, s, w in chunks]
     gs = []
@@ -647,19 +654,22 @@
     chunks = chunk_cols(weights, d)
     n = len(chunks) + 1
     res = residual_shapes(b, t, d, kp, ff)
-    blocks = [gains.shape] + [(weights[i].shape[0], w) for i, _, w in chunks]
+    block = (weights[0].shape[0], LANES)
+    blocks = [block] + [(weights[i].shape[0], w) for i, _, w in chunks]
     fulls = [jax.ShapeDtypeStruct((nz, 2, 2, 2, *s), bf16) for s in blocks]
     count = Gather.count(nz)
     hbm, vm = pl.BlockSpec(memory_space=HBM), pl.BlockSpec(memory_space=VMEM)
     outs = pl.pallas_call(
         functools.partial(forward_kernel, nz, (b, t, d, kp, ff), chunks),
         out_shape=[jax.ShapeDtypeStruct((b * t, d), bf16), *res, *fulls],
-        in_specs=[vm, vm, *([hbm] * 9)],
+        in_specs=[*([vm] * 5), *([hbm] * 8)],
         out_specs=[vm, *([hbm] * (N_RES + n))],
         scratch_shapes=[
             *(pltpu.VMEM(s.shape, s.dtype) for s in (*res, *fulls)),
             pltpu.VMEM((b, *images.shape[1:]), bf16),
             pltpu.VMEM((b + -b % 8, kp), f32),
+            pltpu.VMEM(block, bf16),
+            pltpu.VMEM((8, LANES), f32),
             pltpu.SemaphoreType.DMA((n,)),
             pltpu.SemaphoreType.DMA((n, count)),
             pltpu.SemaphoreType.DMA((n, count)),
@@ -669,7 +679,7 @@
         compiler_params=pltpu.CompilerParams(
             collective_id=0, has_side_effects=True, vmem_limit_bytes=60 << 20
         ),
-    )(xs.reshape(b * t, d), mask, images, gains, *weights)
+    )(xs.reshape(b * t, d), mask, *gains, images, *weights)
     return outs[0], outs[1 : 1 + N_RES], outs[1 + N_RES :]
 
 
@@ -953,7 +963,7 @@
 
 
 PLANES = (0, 3)
-BROAD = ()
+BROAD = (8, 9, 10, 11)
 
 RES_NAMES = (
     "n1", "qkv", "p1", "o1", "x1", "n2", "q2", "kv2",
@@ -1197,10 +1207,7 @@
         gains = jnp.stack([gain_self, gain_cross, gain_mlp], axis=1)
         return native(captions, img, mask, gains, weights, cotangent)
     nz = n_dp // 2
-    lane = lax.broadcasted_iota(jnp.int32, (gain_self.shape[0], LANES), 1)
-    gains = jnp.zeros(lane.shape, bf16)
-    for i, gain in enumerate((gain_self, gain_cross, gain_mlp)):
-        gains = jnp.where(lane == i, gain[:, None], gains)
+    gains = (gain_self, gain_cross, gain_mlp)
     out, res, fulls = forward(nz, captions, images, tissue_mask, gains, weights)
     gx, gimg, *gw, gg = backward(nz, cotangent, patches, captions, weights, res, fulls[1:])
     gimg = gimg.reshape(4 * b, *gimg.shape[2:])

time: 220 us -> 215 us (0.977)
  Pallas kernels: 217 us -> 214 us
    pallas_call x1, Pallas kernels: 114 us -> 110 us  [backward(): pl.pallas_call(functools.partial(backward_kernel, nz, (b, t, d, kp, ff),...]
where the time goes in v1:
time: 215 us
  Pallas kernels  214 us (100%)
    pallas_call x1, Pallas kernels, backward(): pl.pallas_call(functools.partial(backward_kernel, nz, (b, t, d, kp, ff),...  110 us
    pallas_call x1, Pallas kernels, forward(): pl.pallas_call(functools.partial(forward_kernel, nz, (b, t, d, kp, ff), c...  98.7 us
    pallas_call x1, Pallas kernels, finish(): pl.pallas_call(functools.partial(finish_kernel, n), out_shape=[*(S(a.shap...  4.93 us

profile of v1, /device:TPU:0, one launch (start us, length us, event | category | flops | bytes accessed | tf_op | source)
XLA Modules:
  0.0 214.8 jit_solution(13657626580869943341)
XLA Ops:
  0.6 98.7 %shard_map.237 = (bf16[384,768]{1,0:T(8,128)(2,1)}, bf16[384,768]{1,0:T(8,128)(2,1)}, bf16[384,2304]{1,0:T(8,128)(2,1)}, bf16[36,128,128]{2,1,0:T(8,128)(2,1)}, ...) custom-call(bf16[384,768]{1,0:T(8,128)(2,1)} %bitcast.6, ...), custom_call_target="tpu_custom_call" | custom-call | tf_op jit(solution)/shard_map/pallas_call | solution.py:662
  99.4 110.3 %shard_map.238 = (f32[384,768]{1,0:T(8,128)}, bf16[4,3,192,208]{3,2,1,0:T(8,128)(2,1)}, f32[24,2304]{1,0:T(8,128)}, f32[24,768]{1,0:T(8,128)}, f32[24,768]{1,0:T...) custom-call(bf16[384,768]{1,0:T(8,128)(2,1)} %bitcast.9, ...), custom_call_target="tpu_custom_call" | custom-call | tf_op jit(solution)/shard_map/pallas_call | solution.py:994
  209.7 4.9 %shard_map.239 = (bf16[384,768]{1,0:T(8,128)(2,1)}, f32[384,768]{1,0:T(8,128)}, f32[24,2304]{1,0:T(8,128)}, f32[24,768]{1,0:T(8,128)}, f32[24,768]{1,0:T(8,128)}...) custom-call(bf16[384,768]{1,0:T(8,128)(2,1)} %get-tuple-element.68.r, ...), custom_call_target="tpu_custom_call" | custom-call | tf_op jit(solution)/shard_map/pallas_call | solution.py:1061

commit v2 on v1

--- a/solution.py
+++ b/solution.py
@@ -305,10 +305,9 @@
 
 class Planner:
     UNIT = {"xy": 0.8, "z": 0.8, "core": 0.1}
-    HOP = 3.0
-
-    def __init__(self, chunks, sizes):
-        self.chunks, self.sizes = chunks, sizes
+
+    def __init__(self, chunks, sizes, hop):
+        self.chunks, self.sizes, self.hop = chunks, sizes, hop
         self.now, self.free = 0.0, dict.fromkeys(self.UNIT, 0.0)
         self.ready, self.queue, self.arrived = {}, [], None
         self.held, self.ahead = [], 0
@@ -329,7 +328,7 @@
             self.emit(i + self.ahead)
         link, amount = load
         self.free[link] = max(self.free[link], self.now) + self.UNIT[link] * amount * size
-        self.ready[i] = (step + 1, self.free[link] + self.HOP)
+        self.ready[i] = (step + 1, self.free[link] + self.hop)
 
     def settle(self):
         while True:
@@ -452,7 +451,7 @@
         kind = GatherPlane if i in (11, 12) else Gather
         gs.append(kind(here, srcs[i], g[i], (ssem.at[i], rsem.at[i]), local.at[i]))
     sizes = [gsh.shape[-1] / d] + [r.shape[-1] * r.shape[-2] / (d * gsh.shape[0]) for r in g[1:]]
-    plan = Planner(gs, sizes)
+    plan = Planner(gs, sizes, 5.0)
     plan.ahead = AHEAD
     plan.held = [i for i in range(AHEAD, n) if i not in (11, 12)]
     for i in range(n):
@@ -770,7 +769,7 @@
         at = broad if i in BROAD else here
         sc.append(kind(at, parts[i], bufs[i], dst[i], (ssem.at[i], rsem.at[i])))
     sizes = [0.2 if k is None else 1.35 if k >= n_c - 3 else 1.0 for k in order]
-    plan = Planner(sc, sizes)
+    plan = Planner(sc, sizes, 3.0)
     smalls = [i for i, k in enumerate(order) if k is not None and k < n_c - 3]
 
     def slot_ready(i):
@@ -963,7 +962,7 @@
 
 
 PLANES = (0, 3)
-BROAD = (8, 9, 10, 11)
+BROAD = (7, 8, 9, 10, 11, 13)
 
 RES_NAMES = (
     "n1", "qkv", "p1", "o1", "x1", "n2", "q2", "kv2",
@@ -1043,9 +1042,9 @@
         p_in[k].wait()
         lax.fori_loop(k * half, (k + 1) * half, widen, 0)
         p_out[k].start()
-    for i in range(n):
-        arrive[i].wait()
-        leave[i].start()
+        for i in range(k * n // 2, (k + 1) * n // 2):
+            arrive[i].wait()
+            leave[i].start()
     row = jnp.transpose(gg[...])
     for k, r in enumerate(gains):
         r[...] = row[k, : r.shape[0]]

time: 215 us -> 210 us (0.977); the launches traced: 215 us -> 206 us
  Pallas kernels: 214 us -> 206 us
    pallas_call x1, Pallas kernels: 110 us -> 102 us  [backward(): pl.pallas_call(functools.partial(backward_kernel, nz, (b, t, d, kp, ff),...]
where the time goes in v2:
time: 210 us; the launch traced here: 206 us
  Pallas kernels  206 us (98%)
    pallas_call x1, Pallas kernels, backward(): pl.pallas_call(functools.partial(backward_kernel, nz, (b, t, d, kp, ff),...  102 us
    pallas_call x1, Pallas kernels, forward(): pl.pallas_call(functools.partial(forward_kernel, nz, (b, t, d, kp, ff), c...  98.7 us
    pallas_call x1, Pallas kernels, finish(): pl.pallas_call(functools.partial(finish_kernel, n), out_shape=[*(S(a.shap...  5 us

profile of v2, /device:TPU:0, one launch (start us, length us, event | category | flops | bytes accessed | tf_op | source)
XLA Modules:
  0.0 206.4 jit_solution(404269029973590356)
XLA Ops:
  0.6 98.7 %shard_map.237 = (bf16[384,768]{1,0:T(8,128)(2,1)}, bf16[384,768]{1,0:T(8,128)(2,1)}, bf16[384,2304]{1,0:T(8,128)(2,1)}, bf16[36,128,128]{2,1,0:T(8,128)(2,1)}, ...) custom-call(bf16[384,768]{1,0:T(8,128)(2,1)} %bitcast.6, ...), custom_call_target="tpu_custom_call" | custom-call | tf_op jit(solution)/shard_map/pallas_call | solution.py:661
  99.4 101.8 %shard_map.238 = (f32[384,768]{1,0:T(8,128)}, bf16[4,3,192,208]{3,2,1,0:T(8,128)(2,1)}, f32[24,2304]{1,0:T(8,128)}, f32[24,768]{1,0:T(8,128)}, f32[24,768]{1,0:T...) custom-call(bf16[384,768]{1,0:T(8,128)(2,1)} %bitcast.9, ...), custom_call_target="tpu_custom_call" | custom-call | tf_op jit(solution)/shard_map/pallas_call | solution.py:993
  201.2 5.0 %shard_map.239 = (bf16[384,768]{1,0:T(8,128)(2,1)}, f32[384,768]{1,0:T(8,128)}, f32[24,2304]{1,0:T(8,128)}, f32[24,768]{1,0:T(8,128)}, f32[24,768]{1,0:T(8,128)}...) custom-call(bf16[384,768]{1,0:T(8,128)(2,1)} %get-tuple-element.68.r, ...), custom_call_target="tpu_custom_call" | custom-call | tf_op jit(solution)/shard_map/pallas_call | solution.py:1060

commit v3 on v2

--- a/solution.py
+++ b/solution.py
@@ -212,9 +212,17 @@
             self.core.start()
         elif i == 1:
             self.core.wait_recv()
-            self.sum_core()
+
+            def side(q):
+                def at(r):
+                    return lambda i: r.at[lax.rem(i, nz), *h.column(lax.div(i, nz), q)]
+
+                add_blocks(2 * nz, at(self.rc), at(self.rc), at(self.own))
+
+            side(1 - h.s)
             for t in self.s:
                 t.start()
+            side(h.s)
             self.core.wait_send()
         elif i == 2:
             for t in self.s:

time: 210 us -> 210 us (level)
  no operation moved by 1% of the time
where the time goes in v3:
time: 210 us; the launch traced here: 207 us
  Pallas kernels  206 us (98%)
    pallas_call x1, Pallas kernels, backward(): pl.pallas_call(functools.partial(backward_kernel, nz, (b, t, d, kp, ff),...  102 us
    pallas_call x1, Pallas kernels, forward(): pl.pallas_call(functools.partial(forward_kernel, nz, (b, t, d, kp, ff), c...  98.7 us
    pallas_call x1, Pallas kernels, finish(): pl.pallas_call(functools.partial(finish_kernel, n), out_shape=[*(S(a.shap...  5 us

profile of v3, /device:TPU:0, one launch (start us, length us, event | category | flops | bytes accessed | tf_op | source)
XLA Modules:
  0.0 206.5 jit_solution(6856160520703580027)
XLA Ops:
  0.6 98.7 %shard_map.237 = (bf16[384,768]{1,0:T(8,128)(2,1)}, bf16[384,768]{1,0:T(8,128)(2,1)}, bf16[384,2304]{1,0:T(8,128)(2,1)}, bf16[36,128,128]{2,1,0:T(8,128)(2,1)}, ...) custom-call(bf16[384,768]{1,0:T(8,128)(2,1)} %bitcast.6, ...), custom_call_target="tpu_custom_call" | custom-call | tf_op jit(solution)/shard_map/pallas_call | solution.py:669
  99.4 101.9 %shard_map.238 = (f32[384,768]{1,0:T(8,128)}, bf16[4,3,192,208]{3,2,1,0:T(8,128)(2,1)}, f32[24,2304]{1,0:T(8,128)}, f32[24,768]{1,0:T(8,128)}, f32[24,768]{1,0:T...) custom-call(bf16[384,768]{1,0:T(8,128)(2,1)} %bitcast.9, ...), custom_call_target="tpu_custom_call" | custom-call | tf_op jit(solution)/shard_map/pallas_call | solution.py:1001
  201.3 5.0 %shard_map.239 = (bf16[384,768]{1,0:T(8,128)(2,1)}, f32[384,768]{1,0:T(8,128)}, f32[24,2304]{1,0:T(8,128)}, f32[24,768]{1,0:T(8,128)}, f32[24,768]{1,0:T(8,128)}...) custom-call(bf16[384,768]{1,0:T(8,128)(2,1)} %get-tuple-element.68.r, ...), custom_call_target="tpu_custom_call" | custom-call | tf_op jit(solution)/shard_map/pallas_call | solution.py:1068
